TPU v7x, 32 devices: a whole 2x2x4 slice. The times are simulated.
32 devices in a mesh: comp: 2 (over y), gx: 4 (over x, core), gy: 4 (over z).
Axes of the slice: x: 2, y: 2, z: 4, core: 2. Of those that a mesh axis runs over, the one named last changes fastest.
Arguments:
- state: float32 [2, 30, 128, 1024], P('comp', None, 'gx', 'gy'), may hold values from -6 to 6
- conduct: float32 [2, 30, 128, 1024], P('comp', None, 'gx', 'gy'), may hold values from 0.3 to 3
- storage: float32 [2], P('comp'), may hold values from 0.05 to 0.5
- surface_source: float32 [2, 128, 1024], P('comp', 'gx', 'gy'), may hold values from -6 to 6
- plant_type: int32 [2, 128, 1024], P('comp', 'gx', 'gy'), may hold values from 0 to 15
- plant_table: float32 [16, 2], replicated, may hold values from 0.3 to 3
- layer_weights: float32 [2, 16, 6], replicated, may hold values from 0.05 to 1
- remap_rows: int32 [2, 128], P('comp', 'gx'), may hold values from 0 to 31
- remap_weights: float32 [2, 1024, 128], P('comp', 'gy'), may hold values from 0 to 1
Outputs:
- new_state: float32 [2, 30, 128, 1024], P('comp', None, 'gx', 'gy')
- exchange_flux: float32 [2, 128, 1024], P('comp', 'gx', 'gy')
All inputs are finite; a program needn't handle non-finite values.
Results may differ from a plain program's by a relative error of at most 0.0003.
Values sent between devices are 32-bit elements; how exact they have to be, the bound alone decides.
No kernel may reach another device: no remote copies, remote signals or barrier semaphores. Data moves between devices by JAX's collectives and lax.ppermute only.
A program may use at most 64 MiB of HBM per device.

v0:
```python
import jax
import jax.numpy as jnp
from jax import lax
from jax.sharding import PartitionSpec as P

NS = 6
PATCH = 128
PLANTS = 16
ITERS = 3


def from_partner(value, axis, distance):
    mask = 2**distance
    pairs = [(source, source ^ mask) for source in range(lax.axis_size(axis))]
    return lax.ppermute(value, axis, pairs)


def extended(block, sides, width):
    for axis, dim in sides:
        count = lax.axis_size(axis)
        forward = [(i, i + 1) for i in range(count - 1)]
        backward = [(target, source) for source, target in forward]
        low = lax.ppermute(
            lax.slice_in_dim(block, block.shape[dim] - width, None, axis=dim), axis, forward
        )
        high = lax.ppermute(lax.slice_in_dim(block, 0, width, axis=dim), axis, backward)
        block = jnp.concatenate([low, block, high], axis=dim)
    return block


def apply_padded(vp, kp):
    v = vp[1:-1, 1:-1, 1:-1]
    kc = kp[1:-1, 1:-1, 1:-1]
    total = jnp.zeros_like(v)
    moves = [(2, 1, 1), (0, 1, 1), (1, 2, 1), (1, 0, 1), (1, 1, 2), (1, 1, 0)]
    for a, b, e in moves:
        vn = vp[a : a + v.shape[0], b : b + v.shape[1], e : e + v.shape[2]]
        kn = kp[a : a + v.shape[0], b : b + v.shape[1], e : e + v.shape[2]]
        total = total + 0.5 * (kc + kn) * (v - vn)
    return total


def pad_levels(field):
    return jnp.pad(field, ((1, 1), (0, 0), (0, 0)))


def least_squares(hmat, beta):
    gram = jnp.sum(hmat[:, :, None] * hmat[:, None, :], axis=0)
    target_vector = beta * hmat[0, :]
    factor = jnp.linalg.cholesky(gram)
    return jax.scipy.linalg.cho_solve((factor, True), target_vector)


def one_hot_types(kinds):
    return (kinds[None, :, :] == jnp.arange(PLANTS)[:, None, None]).astype(jnp.float32)


def forcing_for(layers, rows, weights, kinds, profile):
    hp = lax.Precision.HIGHEST
    picked = jnp.take(layers, rows, axis=1)
    width = layers.shape[2]
    blocks = picked.reshape(layers.shape[0], layers.shape[1], width // PATCH, PATCH)
    wblk = weights.reshape(width // PATCH, PATCH, PATCH)
    remapped = jnp.einsum("lxbk,bjk->lxbj", blocks, wblk, precision=hp).reshape(layers.shape)
    prof = jnp.einsum("pl,pxy->lxy", profile, one_hot_types(kinds), precision=hp)
    return jnp.sum(prof * remapped, axis=0)


def body(
    state,
    conduct,
    storage,
    surface_source,
    plant_type,
    plant_table,
    layer_weights,
    remap_rows,
    remap_weights,
):
    hp = lax.Precision.HIGHEST
    comp_index = lax.axis_index("comp")
    field = state[0]
    levels = field.shape[0]
    keff = conduct[0] * (1.0 + 0.5 * jnp.tanh(field))
    kinds = plant_type[0]
    own_table = jnp.where(comp_index == 0, layer_weights[0], layer_weights[1])
    other_table = jnp.where(comp_index == 0, layer_weights[1], layer_weights[0])
    layers = field[:NS]
    partner_layers = from_partner(layers, "comp", 0)
    other_force = forcing_for(partner_layers, remap_rows[0], remap_weights[0], kinds, other_table)
    selector = one_hot_types(kinds)
    own_prof = jnp.einsum("pl,pxy->lxy", own_table, selector, precision=hp)
    own_force = jnp.sum(own_prof * layers, axis=0)
    atmospheric_forcing = jnp.where(comp_index == 0, own_force, other_force)
    soil_force = jnp.where(comp_index == 0, other_force, own_force)
    params = jnp.einsum("pq,pxy->qxy", plant_table, selector, precision=hp)
    flux = params[0] * (params[1] * soil_force - atmospheric_forcing)
    sign = 1.0 - 2.0 * comp_index.astype(jnp.float32)
    top = sign * flux[None] * own_prof
    source = jnp.concatenate([top, jnp.zeros((levels - NS,) + flux.shape, jnp.float32)], axis=0)
    source = source.at[0].add(surface_source[0])
    diagonal_shift = storage[0]
    depth = 1
    stacked = jnp.stack([field, keff])
    padded = extended(stacked, (("gx", 2), ("gy", 3)), depth)
    kext = padded[1]

    def apply_extended_operator(vector):
        return apply_padded(pad_levels(vector), pad_levels(kext))

    rhs_rim = 0
    rhs = source - apply_extended_operator(padded[0])
    beta = jnp.sqrt(lax.psum(jnp.sum(rhs * rhs), ("gx", "gy")))
    basis = [rhs / beta]
    rims = [rhs_rim]
    hmat = jnp.zeros((ITERS + 1, ITERS), jnp.float32)
    for j in range(ITERS):
        operate_vector = basis[j]
        padded_vector = extended(operate_vector, (("gx", 1), ("gy", 2)), 1)
        krylov_vector = diagonal_shift * operate_vector + apply_extended_operator(padded_vector)
        near = [basis[i] for i in range(j + 1)]
        interior_vector = krylov_vector
        partials = jnp.stack([jnp.sum(interior_vector * near[i]) for i in range(j + 1)])
        heights, squared = lax.psum(
            (partials, jnp.sum(interior_vector * interior_vector)), ("gx", "gy")
        )
        for i in range(j + 1):
            krylov_vector = krylov_vector - heights[i] * near[i]
            hmat = hmat.at[i, j].set(heights[i])
        nrm = jnp.sqrt(squared - jnp.sum(heights * heights))
        hmat = hmat.at[j + 1, j].set(nrm)
        if j + 1 < ITERS:
            basis.append(krylov_vector / nrm)
            rims.append(0)
    coef = least_squares(hmat, beta)
    update = field
    for j in range(ITERS):
        update = update + coef[j] * basis[j]
    return (update[None], flux[None])


def solution(mesh):
    in_specs = (
        P("comp", None, "gx", "gy"),
        P("comp", None, "gx", "gy"),
        P("comp"),
        P("comp", "gx", "gy"),
        P("comp", "gx", "gy"),
        P(),
        P(),
        P("comp", "gx"),
        P("comp", "gy", None),
    )
    out_specs = (P("comp", None, "gx", "gy"), P("comp", "gx", "gy"))
    return jax.shard_map(body, mesh=mesh, in_specs=in_specs, out_specs=out_specs, check_vma=False)
```

profile of v0, /device:TPU:0, one launch (start us, length us, event | category | flops | bytes accessed | tf_op | source)
XLA Modules:
  0.0 289.8 jit_solution(18306534450903827338)
XLA Ops:
  2.5 3.1 %collective-permute-start = (f32[6,32,256]{2,0,1:T(8,128)}, f32[6,32,256]{2,0,1:T(8,128)}, u32[]{:S(2)}, u32[]{:S(2)}) collective-permute-start(f32[6,32,256]{2,0,1:T(8,128)} %bitcast.108), channel_id=1, source_target_pairs={{0,16},{16,0},{1,17},{17,1},{2,18},{18,2},{3,19},{19,3},{4,20},{20... | collective-permute-start | bytes 589832 | tf_op jit(solution)/shard_map/ppermute | solution.py:15
  15.3 1.8 copy.131
  17.1 4.1 %collective-permute-start.3 = (f32[2,30,34,1]{2,0,3,1:T(2,128)S(1)}, f32[2,30,34,1]{2,0,3,1:T(2,128)}, u32[]{:S(2)}, u32[]{:S(2)}) collective-permute-start(f32[2,30,34,1]{2,0,3,1:T(2,128)S(1)} %copy.131), channel_id=1, source_target_pairs={{0,1},{1,2},{2,3},{4,5},{5,6},{6,7},{8,9},{9,10},{10,11},{12,13},{... | collective-permute-start | bytes 24488 | tf_op jit(solution)/shard_map/ppermute | solution.py:23
  26.2 2.2 collective-permute-done.4
  28.4 2.3 copy.134
  30.7 3.2 %pad_maximum_fusion = f32[2,30,34,258]{3,2,1,0:T(8,128)S(1)} fusion(f32[2,30,34,1]{3,2,1,0:T(8,128)} %copy.134, f32[2,30,1,256]{3,2,1,0:T(1,128)S(1)} %collective-permute-done.2, f32[1,30,32,256]{3,2,1,0:T(8,128)S(1)} %add_multiply_fusion, f32[1,30,32,256]{3,2,1,0:T(8,128)S(1)} %copy-done.2, f32[2,30,1,256]{3,2,1,0:T(1,128)S(1)} %collective-permute-done.1, ...), kind=kLoop, calls=%fused_computation.1 | loop fusion | flops 2631600 | bytes 4210560 | tf_op jit(solution)/shard_map/concatenate | solution.py:27
  35.4 1.7 gather_fusion
  39.7 5.6 %multiply_reduce_fusion.9 = (f32[]{:T(128)}, f32[30,32,256]{2,1,0:T(8,128)S(1)}, f32[30,32,256]{2,1,0:T(8,128)}, f32[30,32,256]{2,1,0:T(8,128)}, f32[30,32,256]{...) fusion(f32[30,32,256]{2,1,0:T(8,128)S(1)} %fusion.80, ...), kind=kLoop, calls=%fused_computation.156 | loop fusion | flops 7864319 | bytes 21381124 | tf_op jit(solution)/shard_map/reduce_sum | solution.py:113
  45.2 34.1 %psum.49 = f32[]{:T(128)} all-reduce(f32[]{:T(128)} %get-tuple-element.149), channel_id=1, replica_groups=mesh['comp'=2,'gx'=4,'gy'=4] {'gx','gy'}, use_global_device_ids=true, to_apply=%region_3.4 | all-reduce | flops 1 | bytes 8 | tf_op jit(solution)/shard_map/psum | solution.py:113
  82.9 4.0 %collective-permute-done.6 = f32[30,1,256]{2,1,0:T(1,128)S(1)} collective-permute-done((f32[30,1,256]{2,1,0:T(1,128)S(1)}, f32[30,1,256]{2,1,0:T(1,128)S(1)}, u32[]{:S(2)}, u32[]{:S(2)}) %collective-permute-start.6) | collective-permute-done | bytes 30752 | tf_op jit(solution)/shard_map/ppermute | solution.py:26
  87.6 2.4 collective-permute-start.7
  93.6 2.3 collective-permute-done.8
  97.1 2.4 select_maximum_fusion.8
  99.6 5.0 %multiply_reduce_fusion.8 = (f32[]{:T(128)}, f32[]{:T(128)}, f32[30,32,256]{2,1,0:T(8,128)}) fusion(f32[30,32,256]{2,1,0:T(8,128)S(1)} %broadcast_divide_fusion, f32[30,32,256]{2,1,0:T(8,128)} %get-tuple-element.156, f32[30,1,256]{2,1,0:T(1,128)S(1)} %collective-permute-done.6, f32[30,1,256]{2,1,0:T(1,128)S(1)} %collective-permute-done.5, ...), kind=kLoop, calls=%fused_computation.155 | loop fusion | flops 7618558 | bytes 9900012 | tf_op jit(solution)/shard_map/reduce_sum | solution.py:123
  104.6 30.7 %all-reduce.9 = (f32[]{:T(128)}, f32[1]{0:T(128)}) all-reduce(f32[]{:T(128)} %get-tuple-element.140, f32[1]{0:T(128)} %bitcast.21), channel_id=1, replica_groups=mesh['comp'=2,'gx'=4,'gy'=4] {'gx','gy'}, use_global_device_ids=true, to_apply=%region_7.8 | all-reduce | flops 2 | bytes 16 | tf_op jit(solution)/shard_map/psum | solution.py:124
  137.3 2.1 subtract_divide_fusion.1
  140.7 3.0 %collective-permute-start.9 = (f32[30,1,256]{2,1,0:T(1,128)S(1)}, f32[30,1,256]{2,1,0:T(1,128)S(1)}, u32[]{:S(2)}, u32[]{:S(2)}) collective-permute-start(f32[30,1,256]{2,1,0:T(1,128)S(1)} %get-tuple-element.173), channel_id=1, source_target_pairs={{0,4},{4,8},{8,12},{1,5},{5,9},{9,13},{2,6},{6,10},{10,14},{3,7},{... | collective-permute-start | bytes 92168 | tf_op jit(solution)/shard_map/ppermute | solution.py:23
  147.4 3.8 %collective-permute-start.11 = (f32[30,34,1]{1,2,0:T(1,128)S(1)}, f32[30,34,1]{1,2,0:T(1,128)S(1)}, u32[]{:S(2)}, u32[]{:S(2)}) collective-permute-start(f32[30,34,1]{1,2,0:T(1,128)S(1)} %copy.141), channel_id=1, source_target_pairs={{0,1},{1,2},{2,3},{4,5},{5,6},{6,7},{8,9},{9,10},{10,11},{12,13},{... | collective-permute-start | bytes 12248 | tf_op jit(solution)/shard_map/ppermute | solution.py:23
  155.7 2.5 collective-permute-done.12
  159.3 2.4 select_maximum_fusion.4
  161.8 4.9 %multiply_reduce_fusion.6 = (f32[]{:T(128)}, f32[]{:T(128)}, f32[]{:T(128)}, f32[30,32,256]{2,1,0:T(8,128)}) fusion(f32[30,32,256]{2,1,0:T(8,128)S(1)} %subtract_divide_fusion.1, f32[30,32,256]{2,1,0:T(8,128)} %get-tuple-element.156, f32[30,1,256]{2,1,0:T(1,128)S(1)} %collective-permute-done.10, f32[30,1,256]{2,1,0:T(1,128)S(1)} %collective-permute-done.9, ...), kind=kLoop, calls=%fused_computation.152 | loop fusion | flops 8355837 | bytes 10883060 | tf_op jit(solution)/shard_map/reduce_sum | solution.py:123
  168.1 30.8 %all-reduce.8 = (f32[]{:T(128)}, f32[2]{0:T(128)S(1)}) all-reduce(f32[]{:T(128)} %get-tuple-element.137, f32[2]{0:T(128)S(1)} %pad_maximum_fusion.31), channel_id=1, replica_groups=mesh['comp'=2,'gx'=4,'gy'=4] {'gx','gy'}, use_global_device_ids=true, to_apply=%region_12.13 | all-reduce | flops 3 | bytes 24 | tf_op jit(solution)/shard_map/psum | solution.py:124
  201.5 2.7 subtract_divide_fusion
  206.9 6.1 %collective-permute-done.14 = f32[30,1,256]{2,1,0:T(1,128)S(1)} collective-permute-done((f32[30,1,256]{2,1,0:T(1,128)S(1)}, f32[30,1,256]{2,1,0:T(1,128)S(1)}, u32[]{:S(2)}, u32[]{:S(2)}) %collective-permute-start.14) | collective-permute-done | bytes 30752 | tf_op jit(solution)/shard_map/ppermute | solution.py:26
  215.8 4.0 %collective-permute-start.15 = (f32[30,34,1]{1,2,0:T(1,128)S(1)}, f32[30,34,1]{1,2,0:T(1,128)S(1)}, u32[]{:S(2)}, u32[]{:S(2)}) collective-permute-start(f32[30,34,1]{1,2,0:T(1,128)S(1)} %copy.147), channel_id=1, source_target_pairs={{0,1},{1,2},{2,3},{4,5},{5,6},{6,7},{8,9},{9,10},{10,11},{12,13},{... | collective-permute-start | bytes 12248 | tf_op jit(solution)/shard_map/ppermute | solution.py:23
  224.5 1.9 scatter.34
  227.3 1.9 dynamic-slice.68
  231.6 2.4 select_maximum_fusion
  234.0 6.0 %multiply_reduce_fusion = (f32[]{:T(128)}, f32[]{:T(128)}, f32[]{:T(128)}, f32[]{:T(128)}) fusion(f32[30,32,256]{2,1,0:T(8,128)} %copy-done.4, f32[30,32,256]{2,1,0:T(8,128)S(1)} %subtract_divide_fusion.1, f32[30,32,256]{2,1,0:T(8,128)} %get-tuple-element.156, f32[30,1,256]{2,1,0:T(1,128)S(1)} %collective-permute-done.14, ...), kind=kLoop, calls=%fused_computation.145 | loop fusion | flops 8847356 | bytes 10883064 | tf_op jit(solution)/shard_map/reduce_sum | solution.py:125
  240.0 1.9 pad_maximum_fusion.32
  242.0 32.9 %all-reduce.7 = (f32[3]{0:T(128)S(1)}, f32[]{:T(128)}) all-reduce(f32[3]{0:T(128)S(1)} %pad_maximum_fusion.32, f32[]{:T(128)} %get-tuple-element.132), channel_id=1, replica_groups=mesh['comp'=2,'gx'=4,'gy'=4] {'gx','gy'}, use_global_device_ids=true, to_apply=%region_18.19 | all-reduce | flops 4 | bytes 32 | tf_op jit(solution)/shard_map/psum | solution.py:124
  285.4 4.4 %fusion.74 = f32[1,30,32,256]{3,2,1,0:T(8,128)} fusion(f32[1,30,32,256]{3,2,1,0:T(8,128)S(1)} %copy-done.3, f32[30,32,256]{2,1,0:T(8,128)} %copy-done.4, f32[30,32,256]{2,1,0:T(8,128)S(1)} %subtract_divide_fusion.1, f32[]{:T(128)} %bitcast.55, f32[]{:T(128)} %bitcast.54, f32[]{:T(128)} %bitcast.53, f32[30,32,256]{2,1,0:T(8,128)S(1)} %get-tuple-element.150, ...), kind=kLoop, calls=%fused_computation.144 | loop fusion | flops 1720320 | bytes 4915216 | tf_op jit(solution)/shard_map/broadcast_in_dim | solution.py:139
  (155 shorter events, 62.0 us)
Async XLA Ops:
  0.6 36.8 %copy-start = (f32[1,256,128]{2,1,0:T(8,128)S(1)}, f32[1,256,128]{2,1,0:T(8,128)}, u32[]{:S(2)}) copy-start(f32[1,256,128]{2,1,0:T(8,128)} %param.37) | copy-start | bytes 393220
  0.6 6.6 %copy-start.2 = (f32[1,30,32,256]{3,2,1,0:T(8,128)S(1)}, f32[1,30,32,256]{3,2,1,0:T(8,128)}, u32[]{:S(2)}) copy-start(f32[1,30,32,256]{3,2,1,0:T(8,128)} %param.29) | copy-start | bytes 2949124
  2.5 7.6 %copy-start.21 = (f32[2,16,6]{1,0,2:T(2,128)S(1)}, f32[2,16,6]{1,0,2:T(2,128)}, u32[]{:S(2)}) copy-start(f32[2,16,6]{1,0,2:T(2,128)} %param.35) | copy-start | bytes 2308
  2.5 7.6 %copy-start.24 = (s32[1,32]{1,0:T(1,128)S(1)}, s32[1,32]{1,0:T(1,128)}, u32[]{:S(2)}) copy-start(s32[1,32]{1,0:T(1,128)} %param.36) | copy-start | bytes 388
  2.5 8.2 %copy-start.18 = (s32[1,32,256]{2,1,0:T(8,128)S(1)}, s32[1,32,256]{2,1,0:T(8,128)}, u32[]{:S(2)}) copy-start(s32[1,32,256]{2,1,0:T(8,128)} %param.33) | copy-start | bytes 98308
  2.5 8.2 %copy-start.23 = (f32[16,2]{0,1:T(2,128)S(1)}, f32[16,2]{0,1:T(2,128)}, u32[]{:S(2)}) copy-start(f32[16,2]{0,1:T(2,128)} %param.34) | copy-start | bytes 388
  2.5 32.9 %collective-permute-start = (f32[6,32,256]{2,0,1:T(8,128)}, f32[6,32,256]{2,0,1:T(8,128)}, u32[]{:S(2)}, u32[]{:S(2)}) collective-permute-start(f32[6,32,256]{2,0,1:T(8,128)} %bitcast.108), channel_id=1, source_target_pairs={{0,16},{16,0},{1,17},{17,1},{2,18},{18,2},{3,19},{19,3},{4,20},{20... | collective-permute-start | bytes 589832 | tf_op jit(solution)/shard_map/ppermute | solution.py:15
  7.4 6.0 %collective-permute-start.1 = (f32[2,30,1,256]{3,2,1,0:T(1,128)S(1)}, f32[2,30,1,256]{3,2,1,0:T(1,128)S(1)}, u32[]{:S(2)}, u32[]{:S(2)}) collective-permute-start(f32[2,30,1,256]{3,2,1,0:T(1,128)S(1)} %get-tuple-element.163), channel_id=1, source_target_pairs={{0,4},{4,8},{8,12},{1,5},{5,9},{9,13},{2,6},{6,10},{10,14},{3,7},{... | collective-permute-start | bytes 184328 | tf_op jit(solution)/shard_map/ppermute | solution.py:23
  8.8 4.7 %collective-permute-start.2 = (f32[2,30,1,256]{3,2,1,0:T(1,128)S(1)}, f32[2,30,1,256]{3,2,1,0:T(1,128)S(1)}, u32[]{:S(2)}, u32[]{:S(2)}) collective-permute-start(f32[2,30,1,256]{3,2,1,0:T(1,128)S(1)} %get-tuple-element.164), channel_id=1, source_target_pairs={{4,0},{8,4},{12,8},{5,1},{9,5},{13,9},{6,2},{10,6},{14,10},{7,3},{... | collective-permute-start | bytes 184328 | tf_op jit(solution)/shard_map/ppermute | solution.py:26
  17.1 7.8 %collective-permute-start.3 = (f32[2,30,34,1]{2,0,3,1:T(2,128)S(1)}, f32[2,30,34,1]{2,0,3,1:T(2,128)}, u32[]{:S(2)}, u32[]{:S(2)}) collective-permute-start(f32[2,30,34,1]{2,0,3,1:T(2,128)S(1)} %copy.131), channel_id=1, source_target_pairs={{0,1},{1,2},{2,3},{4,5},{5,6},{6,7},{8,9},{9,10},{10,11},{12,13},{... | collective-permute-start | bytes 24488 | tf_op jit(solution)/shard_map/ppermute | solution.py:23
  22.3 6.1 %collective-permute-start.4 = (f32[2,30,34,1]{2,0,3,1:T(2,128)}, f32[2,30,34,1]{2,0,3,1:T(2,128)}, u32[]{:S(2)}, u32[]{:S(2)}) collective-permute-start(f32[2,30,34,1]{2,0,3,1:T(2,128)} %copy.132), channel_id=1, source_target_pairs={{1,0},{2,1},{3,2},{5,4},{6,5},{7,6},{9,8},{10,9},{11,10},{13,12},{... | collective-permute-start | bytes 24488 | tf_op jit(solution)/shard_map/ppermute | solution.py:26
  33.9 3.3 %copy-start.22 = (pred[32]{0:T(512)(128)(4,1)S(1)}, pred[32]{0:T(512)(128)(4,1)}, u32[]{:S(2)}) copy-start(pred[32]{0:T(512)(128)(4,1)} %compare_and_fusion) | copy-start | bytes 100
  35.4 3.1 %copy-start.19 = (f32[2,32,256]{2,0,1:T(2,128)S(1)}, f32[2,32,256]{2,0,1:T(2,128)}, u32[]{:S(2)}) copy-start(f32[2,32,256]{2,0,1:T(2,128)} %convolution_bitcast_fusion.1) | copy-start | bytes 196612
  35.4 3.2 %copy-start.17 = (f32[6,32,256]{2,0,1:T(8,128)S(1)}, f32[6,32,256]{2,0,1:T(8,128)}, u32[]{:S(2)}) copy-start(f32[6,32,256]{2,0,1:T(8,128)} %get-tuple-element.194) | copy-start | bytes 589828
  80.3 2.6 collective-permute-start.5
  81.6 5.3 %collective-permute-start.6 = (f32[30,1,256]{2,1,0:T(1,128)S(1)}, f32[30,1,256]{2,1,0:T(1,128)S(1)}, u32[]{:S(2)}, u32[]{:S(2)}) collective-permute-start(f32[30,1,256]{2,1,0:T(1,128)S(1)} %get-tuple-element.176), channel_id=1, source_target_pairs={{4,0},{8,4},{12,8},{5,1},{9,5},{13,9},{6,2},{10,6},{14,10},{7,3},{... | collective-permute-start | bytes 92168 | tf_op jit(solution)/shard_map/ppermute | solution.py:26
  87.6 4.9 %collective-permute-start.7 = (f32[30,34,1]{1,2,0:T(1,128)S(1)}, f32[30,34,1]{1,2,0:T(1,128)S(1)}, u32[]{:S(2)}, u32[]{:S(2)}) collective-permute-start(f32[30,34,1]{1,2,0:T(1,128)S(1)} %copy.135), channel_id=1, source_target_pairs={{0,1},{1,2},{2,3},{4,5},{5,6},{6,7},{8,9},{9,10},{10,11},{12,13},{... | collective-permute-start | bytes 12248 | tf_op jit(solution)/shard_map/ppermute | solution.py:23
  90.3 5.6 %collective-permute-start.8 = (f32[30,34,1]{1,2,0:T(1,128)S(1)}, f32[30,34,1]{1,2,0:T(1,128)S(1)}, u32[]{:S(2)}, u32[]{:S(2)}) collective-permute-start(f32[30,34,1]{1,2,0:T(1,128)S(1)} %copy.136), channel_id=1, source_target_pairs={{1,0},{2,1},{3,2},{5,4},{6,5},{7,6},{9,8},{10,9},{11,10},{13,12},{... | collective-permute-start | bytes 12248 | tf_op jit(solution)/shard_map/ppermute | solution.py:26
  97.1 2.5 copy-start.13
  104.6 39.2 %copy-start.25 = (s32[2]{0:T(128)S(1)}, s32[2]{0:T(128)}, u32[]{:S(2)}) copy-start(s32[2]{0:T(128)} %constant.341.clone.1) | copy-start | bytes 28
  139.4 5.0 %collective-permute-start.10 = (f32[30,1,256]{2,1,0:T(1,128)S(1)}, f32[30,1,256]{2,1,0:T(1,128)S(1)}, u32[]{:S(2)}, u32[]{:S(2)}) collective-permute-start(f32[30,1,256]{2,1,0:T(1,128)S(1)} %get-tuple-element.174), channel_id=1, source_target_pairs={{4,0},{8,4},{12,8},{5,1},{9,5},{13,9},{6,2},{10,6},{14,10},{7,3},{... | collective-permute-start | bytes 92168 | tf_op jit(solution)/shard_map/ppermute | solution.py:26
  140.7 3.9 %collective-permute-start.9 = (f32[30,1,256]{2,1,0:T(1,128)S(1)}, f32[30,1,256]{2,1,0:T(1,128)S(1)}, u32[]{:S(2)}, u32[]{:S(2)}) collective-permute-start(f32[30,1,256]{2,1,0:T(1,128)S(1)} %get-tuple-element.173), channel_id=1, source_target_pairs={{0,4},{4,8},{8,12},{1,5},{5,9},{9,13},{2,6},{6,10},{10,14},{3,7},{... | collective-permute-start | bytes 92168 | tf_op jit(solution)/shard_map/ppermute | solution.py:23
  147.4 7.2 %collective-permute-start.11 = (f32[30,34,1]{1,2,0:T(1,128)S(1)}, f32[30,34,1]{1,2,0:T(1,128)S(1)}, u32[]{:S(2)}, u32[]{:S(2)}) collective-permute-start(f32[30,34,1]{1,2,0:T(1,128)S(1)} %copy.141), channel_id=1, source_target_pairs={{0,1},{1,2},{2,3},{4,5},{5,6},{6,7},{8,9},{9,10},{10,11},{12,13},{... | collective-permute-start | bytes 12248 | tf_op jit(solution)/shard_map/ppermute | solution.py:23
  152.6 5.6 %collective-permute-start.12 = (f32[30,34,1]{1,2,0:T(1,128)S(1)}, f32[30,34,1]{1,2,0:T(1,128)S(1)}, u32[]{:S(2)}, u32[]{:S(2)}) collective-permute-start(f32[30,34,1]{1,2,0:T(1,128)S(1)} %copy.142), channel_id=1, source_target_pairs={{1,0},{2,1},{3,2},{5,4},{6,5},{7,6},{9,8},{10,9},{11,10},{13,12},{... | collective-permute-start | bytes 12248 | tf_op jit(solution)/shard_map/ppermute | solution.py:26
  159.3 2.5 copy-start.16
  204.3 27.3 %copy-start.4 = (f32[30,32,256]{2,1,0:T(8,128)}, f32[30,32,256]{2,1,0:T(8,128)S(1)}, u32[]{:S(2)}) copy-start(f32[30,32,256]{2,1,0:T(8,128)S(1)} %subtract_divide_fusion) | copy-start | bytes 2949124
  204.3 2.6 collective-permute-start.13
  205.6 7.4 %collective-permute-start.14 = (f32[30,1,256]{2,1,0:T(1,128)S(1)}, f32[30,1,256]{2,1,0:T(1,128)S(1)}, u32[]{:S(2)}, u32[]{:S(2)}) collective-permute-start(f32[30,1,256]{2,1,0:T(1,128)S(1)} %get-tuple-element.172), channel_id=1, source_target_pairs={{4,0},{8,4},{12,8},{5,1},{9,5},{13,9},{6,2},{10,6},{14,10},{7,3},{... | collective-permute-start | bytes 92168 | tf_op jit(solution)/shard_map/ppermute | solution.py:26
  215.8 13.4 %collective-permute-start.15 = (f32[30,34,1]{1,2,0:T(1,128)S(1)}, f32[30,34,1]{1,2,0:T(1,128)S(1)}, u32[]{:S(2)}, u32[]{:S(2)}) collective-permute-start(f32[30,34,1]{1,2,0:T(1,128)S(1)} %copy.147), channel_id=1, source_target_pairs={{0,1},{1,2},{2,3},{4,5},{5,6},{6,7},{8,9},{9,10},{10,11},{12,13},{... | collective-permute-start | bytes 12248 | tf_op jit(solution)/shard_map/ppermute | solution.py:23
  221.2 9.2 %collective-permute-start.16 = (f32[30,34,1]{1,2,0:T(1,128)S(1)}, f32[30,34,1]{1,2,0:T(1,128)S(1)}, u32[]{:S(2)}, u32[]{:S(2)}) collective-permute-start(f32[30,34,1]{1,2,0:T(1,128)S(1)} %copy.148), channel_id=1, source_target_pairs={{1,0},{2,1},{3,2},{5,4},{6,5},{7,6},{9,8},{10,9},{11,10},{13,12},{... | collective-permute-start | bytes 12248 | tf_op jit(solution)/shard_map/ppermute | solution.py:26
  231.6 2.5 copy-start.15
  234.0 51.3 %copy-start.3 = (f32[1,30,32,256]{3,2,1,0:T(8,128)S(1)}, f32[1,30,32,256]{3,2,1,0:T(8,128)}, u32[]{:S(2)}) copy-start(f32[1,30,32,256]{3,2,1,0:T(8,128)} %param.29) | copy-start | bytes 2949124
  (11 other events, 24.4 us)
where the time goes:
time: 291 us; the launch traced here: 290 us
  blocking collectives  129 us (44%)
  other arithmetic  53.6 us (18%)
  local copies, waits for them, and re-layouts  43 us (15%)
  starting transfers between devices  35 us (12%)
  waiting for transfers between devices  17.6 us (6%)
  between operations  9.11 us (3%)
  matrix products  2.96 us (1%)
    psum x3, blocking collectives, body(): lax.psum((partials, jnp.sum(interior_vector * interior_vector)), ('gx', '...  94.4 us
    psum x1, blocking collectives, body(): beta = jnp.sqrt(lax.psum(jnp.sum(rhs * rhs), ('gx', 'gy')))  34.1 us
    ppermute x8, starting transfers between devices, extended(): lax.ppermute(lax.slice_in_dim(block, block.shape[dim] - width, None, axis...  21.4 us
    ppermute x8, waiting for transfers between devices, extended(): lax.ppermute(lax.slice_in_dim(block, 0, width, axis=dim), axis, backward)  17.3 us
    concatenate x8, other arithmetic, extended(): block = jnp.concatenate([low, block, high], axis=dim)  11.1 us
    ppermute x8, starting transfers between devices, extended(): lax.ppermute(lax.slice_in_dim(block, 0, width, axis=dim), axis, backward)  10.5 us
    reduce_sum x2, other arithmetic, body(): jnp.sum(interior_vector * near[i])  9.97 us
    slice x7, local copies, waits for them, and re-layouts, extended(): lax.slice_in_dim(block, 0, width, axis=dim)  6.84 us
  transfers between devices with their start and end apart: 17, of which 7 were waited for; matrix products, arithmetic and copies ran while one was open for 12% of the time, Pallas kernels for 0%

commit v1 on v0

--- a/solution.py
+++ b/solution.py
@@ -7,6 +7,11 @@
 PATCH = 128
 PLANTS = 16
 ITERS = 3
+
+
+def by_each_axis(value_2, one, other):
+    half = lax.psum(value_2, one)
+    return lax.psum(half, other)
 
 
 def from_partner(value, axis, distance):
@@ -121,8 +126,8 @@
         near = [basis[i] for i in range(j + 1)]
         interior_vector = krylov_vector
         partials = jnp.stack([jnp.sum(interior_vector * near[i]) for i in range(j + 1)])
-        heights, squared = lax.psum(
-            (partials, jnp.sum(interior_vector * interior_vector)), ("gx", "gy")
+        heights, squared = by_each_axis(
+            (partials, jnp.sum(interior_vector * interior_vector)), "gy", "gx"
         )
         for i in range(j + 1):
             krylov_vector = krylov_vector - heights[i] * near[i]

time: 291 us -> 246 us (0.85)
  blocking collectives: 129 us -> 86 us
    psum x3 -> x6, blocking collectives: 94.4 us -> 51.9 us  [the longest x3 30.1 us: by_each_axis(): half = lax.psum(value_2, one)]
  transfers between devices with their start and end apart: 17 -> 17, of which waited for: 7 -> 7; matrix products, arithmetic and copies ran while one was open for 12% -> 14% of each run, Pallas kernels for 0% -> 0%
where the time goes in v1:
time: 246 us; the launch traced here: 245 us
  blocking collectives  86 us (35%)
  other arithmetic  53.8 us (22%)
  local copies, waits for them, and re-layouts  42.8 us (17%)
  starting transfers between devices  35.3 us (14%)
  waiting for transfers between devices  14.7 us (6%)
  between operations  9.2 us (4%)
  matrix products  2.95 us (1%)
    psum x1, blocking collectives, body(): beta = jnp.sqrt(lax.psum(jnp.sum(rhs * rhs), ('gx', 'gy')))  34.1 us
    psum x3, blocking collectives, by_each_axis(): half = lax.psum(value_2, one)  30.1 us
    ppermute x8, starting transfers between devices, extended(): lax.ppermute(lax.slice_in_dim(block, block.shape[dim] - width, None, axis...  21.8 us
    psum x3, blocking collectives, by_each_axis(): return lax.psum(half, other)  21.7 us
    ppermute x8, waiting for transfers between devices, extended(): lax.ppermute(lax.slice_in_dim(block, 0, width, axis=dim), axis, backward)  14.6 us
    concatenate x8, other arithmetic, extended(): block = jnp.concatenate([low, block, high], axis=dim)  11.1 us
    ppermute x8, starting transfers between devices, extended(): lax.ppermute(lax.slice_in_dim(block, 0, width, axis=dim), axis, backward)  10.5 us
    reduce_sum x2, other arithmetic, body(): jnp.sum(interior_vector * near[i])  10 us
  transfers between devices with their start and end apart: 17, of which 7 were waited for; matrix products, arithmetic and copies ran while one was open for 14% of the time, Pallas kernels for 0%

profile of v1, /device:TPU:0, one launch (start us, length us, event | category | flops | bytes accessed | tf_op | source)
XLA Modules:
  0.0 244.8 jit_solution(15109669030849163453)
XLA Ops:
  2.5 3.1 %collective-permute-start = (f32[6,32,256]{2,0,1:T(8,128)}, f32[6,32,256]{2,0,1:T(8,128)}, u32[]{:S(2)}, u32[]{:S(2)}) collective-permute-start(f32[6,32,256]{2,0,1:T(8,128)} %bitcast.108), channel_id=1, source_target_pairs={{0,16},{16,0},{1,17},{17,1},{2,18},{18,2},{3,19},{19,3},{4,20},{20... | collective-permute-start | bytes 589832 | tf_op jit(solution)/shard_map/ppermute | solution.py:20
  17.1 4.1 %collective-permute-start.3 = (f32[2,30,34,1]{2,0,3,1:T(2,128)S(1)}, f32[2,30,34,1]{2,0,3,1:T(2,128)}, u32[]{:S(2)}, u32[]{:S(2)}) collective-permute-start(f32[2,30,34,1]{2,0,3,1:T(2,128)S(1)} %copy.131), channel_id=1, source_target_pairs={{0,1},{1,2},{2,3},{4,5},{5,6},{6,7},{8,9},{9,10},{10,11},{12,13},{... | collective-permute-start | bytes 24488 | tf_op jit(solution)/shard_map/ppermute | solution.py:28
  26.2 2.2 collective-permute-done.4
  28.4 2.3 copy.134
  30.8 3.2 %pad_maximum_fusion = f32[2,30,34,258]{3,2,1,0:T(8,128)S(1)} fusion(f32[2,30,34,1]{3,2,1,0:T(8,128)} %copy.134, f32[2,30,1,256]{3,2,1,0:T(1,128)S(1)} %collective-permute-done.2, f32[1,30,32,256]{3,2,1,0:T(8,128)S(1)} %add_multiply_fusion, f32[1,30,32,256]{3,2,1,0:T(8,128)S(1)} %copy-done.2, f32[2,30,1,256]{3,2,1,0:T(1,128)S(1)} %collective-permute-done.1, ...), kind=kLoop, calls=%fused_computation.1 | loop fusion | flops 2631600 | bytes 4210560 | tf_op jit(solution)/shard_map/concatenate | solution.py:32
  39.7 5.6 %multiply_reduce_fusion.9 = (f32[]{:T(128)}, f32[30,32,256]{2,1,0:T(8,128)S(1)}, f32[30,32,256]{2,1,0:T(8,128)}, f32[30,32,256]{2,1,0:T(8,128)}, f32[30,32,256]{...) fusion(f32[30,32,256]{2,1,0:T(8,128)S(1)} %fusion.80, ...), kind=kLoop, calls=%fused_computation.156 | loop fusion | flops 7864319 | bytes 21381124 | tf_op jit(solution)/shard_map/reduce_sum | solution.py:118
  45.3 34.1 %psum.91 = f32[]{:T(128)} all-reduce(f32[]{:T(128)} %get-tuple-element.155), channel_id=1, replica_groups=mesh['comp'=2,'gx'=4,'gy'=4] {'gx','gy'}, use_global_device_ids=true, to_apply=%region_3.4 | all-reduce | flops 1 | bytes 8 | tf_op jit(solution)/shard_map/psum | solution.py:118
  82.9 4.0 %collective-permute-done.6 = f32[30,1,256]{2,1,0:T(1,128)S(1)} collective-permute-done((f32[30,1,256]{2,1,0:T(1,128)S(1)}, f32[30,1,256]{2,1,0:T(1,128)S(1)}, u32[]{:S(2)}, u32[]{:S(2)}) %collective-permute-start.6) | collective-permute-done | bytes 30752 | tf_op jit(solution)/shard_map/ppermute | solution.py:31
  87.6 2.4 collective-permute-start.7
  93.6 2.3 collective-permute-done.8
  97.1 2.4 select_maximum_fusion.8
  99.6 5.1 %multiply_reduce_fusion.8 = (f32[]{:T(128)}, f32[]{:T(128)}, f32[30,32,256]{2,1,0:T(8,128)}) fusion(f32[30,32,256]{2,1,0:T(8,128)S(1)} %broadcast_divide_fusion, f32[30,32,256]{2,1,0:T(8,128)} %get-tuple-element.162, f32[30,1,256]{2,1,0:T(1,128)S(1)} %collective-permute-done.6, f32[30,1,256]{2,1,0:T(1,128)S(1)} %collective-permute-done.5, ...), kind=kLoop, calls=%fused_computation.155 | loop fusion | flops 7618558 | bytes 9900012 | tf_op jit(solution)/shard_map/reduce_sum | solution.py:128
  104.7 9.4 %all-reduce.9 = (f32[]{:T(128)}, f32[1]{0:T(128)}) all-reduce(f32[]{:T(128)} %get-tuple-element.140, f32[1]{0:T(128)} %bitcast.21), channel_id=1, replica_groups=mesh['comp'=2,'gx'=4,'gy'=4] {'gy'}, use_global_device_ids=true, to_apply=%region_8.9 | all-reduce | flops 2 | bytes 16 | tf_op jit(solution)/shard_map/psum | solution.py:13
  114.0 6.7 %all-reduce.12 = (f32[]{:T(128)}, f32[1]{0:T(128)}) all-reduce(f32[]{:T(128)} %get-tuple-element.145, f32[1]{0:T(128)} %get-tuple-element.146), channel_id=1, replica_groups=mesh['comp'=2,'gx'=4,'gy'=4] {'gx'}, use_global_device_ids=true, to_apply=%region_9.10 | all-reduce | flops 2 | bytes 16 | tf_op jit(solution)/shard_map/psum | solution.py:14
  122.7 2.0 subtract_divide_fusion.1
  126.1 3.0 %collective-permute-start.9 = (f32[30,1,256]{2,1,0:T(1,128)S(1)}, f32[30,1,256]{2,1,0:T(1,128)S(1)}, u32[]{:S(2)}, u32[]{:S(2)}) collective-permute-start(f32[30,1,256]{2,1,0:T(1,128)S(1)} %get-tuple-element.179), channel_id=1, source_target_pairs={{0,4},{4,8},{8,12},{1,5},{5,9},{9,13},{2,6},{6,10},{10,14},{3,7},{... | collective-permute-start | bytes 92168 | tf_op jit(solution)/shard_map/ppermute | solution.py:28
  132.7 3.6 %collective-permute-start.11 = (f32[30,34,1]{1,2,0:T(1,128)S(1)}, f32[30,34,1]{1,2,0:T(1,128)S(1)}, u32[]{:S(2)}, u32[]{:S(2)}) collective-permute-start(f32[30,34,1]{1,2,0:T(1,128)S(1)} %copy.141), channel_id=1, source_target_pairs={{0,1},{1,2},{2,3},{4,5},{5,6},{6,7},{8,9},{9,10},{10,11},{12,13},{... | collective-permute-start | bytes 12248 | tf_op jit(solution)/shard_map/ppermute | solution.py:28
  140.7 2.5 %collective-permute-done.12 = f32[30,34,1]{1,2,0:T(1,128)S(1)} collective-permute-done((f32[30,34,1]{1,2,0:T(1,128)S(1)}, f32[30,34,1]{1,2,0:T(1,128)S(1)}, u32[]{:S(2)}, u32[]{:S(2)}) %collective-permute-start.12) | collective-permute-done | bytes 4112 | tf_op jit(solution)/shard_map/ppermute | solution.py:31
  144.4 2.4 select_maximum_fusion.4
  146.9 5.0 %multiply_reduce_fusion.6 = (f32[]{:T(128)}, f32[]{:T(128)}, f32[]{:T(128)}, f32[30,32,256]{2,1,0:T(8,128)}) fusion(f32[30,32,256]{2,1,0:T(8,128)S(1)} %subtract_divide_fusion.1, f32[30,32,256]{2,1,0:T(8,128)} %get-tuple-element.162, f32[30,1,256]{2,1,0:T(1,128)S(1)} %collective-permute-done.10, f32[30,1,256]{2,1,0:T(1,128)S(1)} %collective-permute-done.9, ...), kind=kLoop, calls=%fused_computation.152 | loop fusion | flops 8355837 | bytes 10883060 | tf_op jit(solution)/shard_map/reduce_sum | solution.py:128
  153.1 9.1 %all-reduce.8 = (f32[]{:T(128)}, f32[2]{0:T(128)S(1)}) all-reduce(f32[]{:T(128)} %get-tuple-element.137, f32[2]{0:T(128)S(1)} %pad_maximum_fusion.31), channel_id=1, replica_groups=mesh['comp'=2,'gx'=4,'gy'=4] {'gy'}, use_global_device_ids=true, to_apply=%region_15.16 | all-reduce | flops 3 | bytes 24 | tf_op jit(solution)/shard_map/psum | solution.py:13
  162.2 8.3 %all-reduce.11 = (f32[]{:T(128)}, f32[2]{0:T(128)S(1)}) all-reduce(f32[]{:T(128)} %get-tuple-element.143, f32[2]{0:T(128)S(1)} %get-tuple-element.144), channel_id=1, replica_groups=mesh['comp'=2,'gx'=4,'gy'=4] {'gx'}, use_global_device_ids=true, to_apply=%region_16.17 | all-reduce | flops 3 | bytes 24 | tf_op jit(solution)/shard_map/psum | solution.py:14
  173.3 2.8 %subtract_divide_fusion = f32[30,32,256]{2,1,0:T(8,128)S(1)} fusion(f32[30,32,256]{2,1,0:T(8,128)S(1)} %subtract_divide_fusion.1, f32[30,32,256]{2,1,0:T(8,128)} %get-tuple-element.153, f32[]{:T(128)} %sqrt.14, f32[]{:T(128)} %bitcast.35, f32[]{:T(128)} %bitcast.34, f32[30,32,256]{2,1,0:T(8,128)S(1)} %get-tuple-element.156, f32[]{:T(128)S(6)} %sqrt.12), kind=kLoop, calls=%fused_computation.149 | loop fusion | flops 1474560 | bytes 3932176 | tf_op jit(solution)/shard_map/div | solution.py:138
  176.1 2.2 collective-permute-start.13
  179.7 3.3 %collective-permute-done.14 = f32[30,1,256]{2,1,0:T(1,128)S(1)} collective-permute-done((f32[30,1,256]{2,1,0:T(1,128)S(1)}, f32[30,1,256]{2,1,0:T(1,128)S(1)}, u32[]{:S(2)}, u32[]{:S(2)}) %collective-permute-start.14) | collective-permute-done | bytes 30752 | tf_op jit(solution)/shard_map/ppermute | solution.py:31
  185.7 3.7 %collective-permute-start.15 = (f32[30,34,1]{1,2,0:T(1,128)S(1)}, f32[30,34,1]{1,2,0:T(1,128)S(1)}, u32[]{:S(2)}, u32[]{:S(2)}) collective-permute-start(f32[30,34,1]{1,2,0:T(1,128)S(1)} %copy.147), channel_id=1, source_target_pairs={{0,1},{1,2},{2,3},{4,5},{5,6},{6,7},{8,9},{9,10},{10,11},{12,13},{... | collective-permute-start | bytes 12248 | tf_op jit(solution)/shard_map/ppermute | solution.py:28
  194.1 2.0 scatter.34
  201.1 2.4 select_maximum_fusion
  203.6 6.0 %multiply_reduce_fusion = (f32[]{:T(128)}, f32[]{:T(128)}, f32[]{:T(128)}, f32[]{:T(128)}) fusion(f32[30,32,256]{2,1,0:T(8,128)} %copy-done.4, f32[30,32,256]{2,1,0:T(8,128)S(1)} %subtract_divide_fusion.1, f32[30,32,256]{2,1,0:T(8,128)} %get-tuple-element.162, f32[30,1,256]{2,1,0:T(1,128)S(1)} %collective-permute-done.14, ...), kind=kLoop, calls=%fused_computation.145 | loop fusion | flops 8847356 | bytes 10883064 | tf_op jit(solution)/shard_map/reduce_sum | solution.py:130
  211.5 11.7 %all-reduce.7 = (f32[3]{0:T(128)S(1)}, f32[]{:T(128)}) all-reduce(f32[3]{0:T(128)S(1)} %pad_maximum_fusion.32, f32[]{:T(128)} %get-tuple-element.132), channel_id=1, replica_groups=mesh['comp'=2,'gx'=4,'gy'=4] {'gy'}, use_global_device_ids=true, to_apply=%region_22.23 | all-reduce | flops 4 | bytes 32 | tf_op jit(solution)/shard_map/psum | solution.py:13
  223.2 6.7 %all-reduce.10 = (f32[3]{0:T(128)S(1)}, f32[]{:T(128)}) all-reduce(f32[3]{0:T(128)S(1)} %get-tuple-element.141, f32[]{:T(128)} %get-tuple-element.142), channel_id=1, replica_groups=mesh['comp'=2,'gx'=4,'gy'=4] {'gx'}, use_global_device_ids=true, to_apply=%region_23.24 | all-reduce | flops 4 | bytes 32 | tf_op jit(solution)/shard_map/psum | solution.py:14
  240.4 4.4 %fusion.74 = f32[1,30,32,256]{3,2,1,0:T(8,128)} fusion(f32[1,30,32,256]{3,2,1,0:T(8,128)S(1)} %copy-done.3, f32[30,32,256]{2,1,0:T(8,128)} %copy-done.4, f32[30,32,256]{2,1,0:T(8,128)S(1)} %subtract_divide_fusion.1, f32[]{:T(128)} %bitcast.55, f32[]{:T(128)} %bitcast.54, f32[]{:T(128)} %bitcast.53, f32[30,32,256]{2,1,0:T(8,128)S(1)} %get-tuple-element.156, ...), kind=kLoop, calls=%fused_computation.144 | loop fusion | flops 1720320 | bytes 4915216 | tf_op jit(solution)/shard_map/broadcast_in_dim | solution.py:144
  (158 shorter events, 67.7 us)
Async XLA Ops:
  0.6 36.8 %copy-start = (f32[1,256,128]{2,1,0:T(8,128)S(1)}, f32[1,256,128]{2,1,0:T(8,128)}, u32[]{:S(2)}) copy-start(f32[1,256,128]{2,1,0:T(8,128)} %param.37) | copy-start | bytes 393220
  0.6 6.6 %copy-start.2 = (f32[1,30,32,256]{3,2,1,0:T(8,128)S(1)}, f32[1,30,32,256]{3,2,1,0:T(8,128)}, u32[]{:S(2)}) copy-start(f32[1,30,32,256]{3,2,1,0:T(8,128)} %param.29) | copy-start | bytes 2949124
  2.5 7.6 %copy-start.21 = (f32[2,16,6]{1,0,2:T(2,128)S(1)}, f32[2,16,6]{1,0,2:T(2,128)}, u32[]{:S(2)}) copy-start(f32[2,16,6]{1,0,2:T(2,128)} %param.35) | copy-start | bytes 2308
  2.5 7.6 %copy-start.24 = (s32[1,32]{1,0:T(1,128)S(1)}, s32[1,32]{1,0:T(1,128)}, u32[]{:S(2)}) copy-start(s32[1,32]{1,0:T(1,128)} %param.36) | copy-start | bytes 388
  2.5 8.2 %copy-start.18 = (s32[1,32,256]{2,1,0:T(8,128)S(1)}, s32[1,32,256]{2,1,0:T(8,128)}, u32[]{:S(2)}) copy-start(s32[1,32,256]{2,1,0:T(8,128)} %param.33) | copy-start | bytes 98308
  2.5 8.2 %copy-start.23 = (f32[16,2]{0,1:T(2,128)S(1)}, f32[16,2]{0,1:T(2,128)}, u32[]{:S(2)}) copy-start(f32[16,2]{0,1:T(2,128)} %param.34) | copy-start | bytes 388
  2.5 32.9 %collective-permute-start = (f32[6,32,256]{2,0,1:T(8,128)}, f32[6,32,256]{2,0,1:T(8,128)}, u32[]{:S(2)}, u32[]{:S(2)}) collective-permute-start(f32[6,32,256]{2,0,1:T(8,128)} %bitcast.108), channel_id=1, source_target_pairs={{0,16},{16,0},{1,17},{17,1},{2,18},{18,2},{3,19},{19,3},{4,20},{20... | collective-permute-start | bytes 589832 | tf_op jit(solution)/shard_map/ppermute | solution.py:20
  7.4 6.0 %collective-permute-start.1 = (f32[2,30,1,256]{3,2,1,0:T(1,128)S(1)}, f32[2,30,1,256]{3,2,1,0:T(1,128)S(1)}, u32[]{:S(2)}, u32[]{:S(2)}) collective-permute-start(f32[2,30,1,256]{3,2,1,0:T(1,128)S(1)} %get-tuple-element.169), channel_id=1, source_target_pairs={{0,4},{4,8},{8,12},{1,5},{5,9},{9,13},{2,6},{6,10},{10,14},{3,7},{... | collective-permute-start | bytes 184328 | tf_op jit(solution)/shard_map/ppermute | solution.py:28
  8.8 4.7 %collective-permute-start.2 = (f32[2,30,1,256]{3,2,1,0:T(1,128)S(1)}, f32[2,30,1,256]{3,2,1,0:T(1,128)S(1)}, u32[]{:S(2)}, u32[]{:S(2)}) collective-permute-start(f32[2,30,1,256]{3,2,1,0:T(1,128)S(1)} %get-tuple-element.170), channel_id=1, source_target_pairs={{4,0},{8,4},{12,8},{5,1},{9,5},{13,9},{6,2},{10,6},{14,10},{7,3},{... | collective-permute-start | bytes 184328 | tf_op jit(solution)/shard_map/ppermute | solution.py:31
  17.1 7.8 %collective-permute-start.3 = (f32[2,30,34,1]{2,0,3,1:T(2,128)S(1)}, f32[2,30,34,1]{2,0,3,1:T(2,128)}, u32[]{:S(2)}, u32[]{:S(2)}) collective-permute-start(f32[2,30,34,1]{2,0,3,1:T(2,128)S(1)} %copy.131), channel_id=1, source_target_pairs={{0,1},{1,2},{2,3},{4,5},{5,6},{6,7},{8,9},{9,10},{10,11},{12,13},{... | collective-permute-start | bytes 24488 | tf_op jit(solution)/shard_map/ppermute | solution.py:28
  22.4 6.1 %collective-permute-start.4 = (f32[2,30,34,1]{2,0,3,1:T(2,128)}, f32[2,30,34,1]{2,0,3,1:T(2,128)}, u32[]{:S(2)}, u32[]{:S(2)}) collective-permute-start(f32[2,30,34,1]{2,0,3,1:T(2,128)} %copy.132), channel_id=1, source_target_pairs={{1,0},{2,1},{3,2},{5,4},{6,5},{7,6},{9,8},{10,9},{11,10},{13,12},{... | collective-permute-start | bytes 24488 | tf_op jit(solution)/shard_map/ppermute | solution.py:31
  33.9 3.3 %copy-start.22 = (pred[32]{0:T(512)(128)(4,1)S(1)}, pred[32]{0:T(512)(128)(4,1)}, u32[]{:S(2)}) copy-start(pred[32]{0:T(512)(128)(4,1)} %compare_and_fusion) | copy-start | bytes 100
  35.5 3.1 %copy-start.19 = (f32[2,32,256]{2,0,1:T(2,128)S(1)}, f32[2,32,256]{2,0,1:T(2,128)}, u32[]{:S(2)}) copy-start(f32[2,32,256]{2,0,1:T(2,128)} %convolution_bitcast_fusion.1) | copy-start | bytes 196612
  35.5 3.2 %copy-start.17 = (f32[6,32,256]{2,0,1:T(8,128)S(1)}, f32[6,32,256]{2,0,1:T(8,128)}, u32[]{:S(2)}) copy-start(f32[6,32,256]{2,0,1:T(8,128)} %get-tuple-element.200) | copy-start | bytes 589828
  80.3 2.6 %collective-permute-start.5 = (f32[30,1,256]{2,1,0:T(1,128)S(1)}, f32[30,1,256]{2,1,0:T(1,128)S(1)}, u32[]{:S(2)}, u32[]{:S(2)}) collective-permute-start(f32[30,1,256]{2,1,0:T(1,128)S(1)} %get-tuple-element.181), channel_id=1, source_target_pairs={{0,4},{4,8},{8,12},{1,5},{5,9},{9,13},{2,6},{6,10},{10,14},{3,7},{... | collective-permute-start | bytes 92168 | tf_op jit(solution)/shard_map/ppermute | solution.py:28
  81.6 5.3 %collective-permute-start.6 = (f32[30,1,256]{2,1,0:T(1,128)S(1)}, f32[30,1,256]{2,1,0:T(1,128)S(1)}, u32[]{:S(2)}, u32[]{:S(2)}) collective-permute-start(f32[30,1,256]{2,1,0:T(1,128)S(1)} %get-tuple-element.182), channel_id=1, source_target_pairs={{4,0},{8,4},{12,8},{5,1},{9,5},{13,9},{6,2},{10,6},{14,10},{7,3},{... | collective-permute-start | bytes 92168 | tf_op jit(solution)/shard_map/ppermute | solution.py:31
  87.6 4.8 %collective-permute-start.7 = (f32[30,34,1]{1,2,0:T(1,128)S(1)}, f32[30,34,1]{1,2,0:T(1,128)S(1)}, u32[]{:S(2)}, u32[]{:S(2)}) collective-permute-start(f32[30,34,1]{1,2,0:T(1,128)S(1)} %copy.135), channel_id=1, source_target_pairs={{0,1},{1,2},{2,3},{4,5},{5,6},{6,7},{8,9},{9,10},{10,11},{12,13},{... | collective-permute-start | bytes 12248 | tf_op jit(solution)/shard_map/ppermute | solution.py:28
  90.3 5.6 %collective-permute-start.8 = (f32[30,34,1]{1,2,0:T(1,128)S(1)}, f32[30,34,1]{1,2,0:T(1,128)S(1)}, u32[]{:S(2)}, u32[]{:S(2)}) collective-permute-start(f32[30,34,1]{1,2,0:T(1,128)S(1)} %copy.136), channel_id=1, source_target_pairs={{1,0},{2,1},{3,2},{5,4},{6,5},{7,6},{9,8},{10,9},{11,10},{13,12},{... | collective-permute-start | bytes 12248 | tf_op jit(solution)/shard_map/ppermute | solution.py:31
  97.1 2.5 %copy-start.13 = (f32[30,32,256]{2,1,0:T(8,128)S(1)}, f32[30,32,256]{2,1,0:T(8,128)}, u32[]{:S(2)}) copy-start(f32[30,32,256]{2,1,0:T(8,128)} %get-tuple-element.160) | copy-start | bytes 2949124
  104.7 24.5 %copy-start.25 = (s32[2]{0:T(128)S(1)}, s32[2]{0:T(128)}, u32[]{:S(2)}) copy-start(s32[2]{0:T(128)} %constant.341.clone.1) | copy-start | bytes 28
  124.8 5.1 %collective-permute-start.10 = (f32[30,1,256]{2,1,0:T(1,128)S(1)}, f32[30,1,256]{2,1,0:T(1,128)S(1)}, u32[]{:S(2)}, u32[]{:S(2)}) collective-permute-start(f32[30,1,256]{2,1,0:T(1,128)S(1)} %get-tuple-element.180), channel_id=1, source_target_pairs={{4,0},{8,4},{12,8},{5,1},{9,5},{13,9},{6,2},{10,6},{14,10},{7,3},{... | collective-permute-start | bytes 92168 | tf_op jit(solution)/shard_map/ppermute | solution.py:31
  126.1 3.9 %collective-permute-start.9 = (f32[30,1,256]{2,1,0:T(1,128)S(1)}, f32[30,1,256]{2,1,0:T(1,128)S(1)}, u32[]{:S(2)}, u32[]{:S(2)}) collective-permute-start(f32[30,1,256]{2,1,0:T(1,128)S(1)} %get-tuple-element.179), channel_id=1, source_target_pairs={{0,4},{4,8},{8,12},{1,5},{5,9},{9,13},{2,6},{6,10},{10,14},{3,7},{... | collective-permute-start | bytes 92168 | tf_op jit(solution)/shard_map/ppermute | solution.py:28
  132.7 6.9 %collective-permute-start.11 = (f32[30,34,1]{1,2,0:T(1,128)S(1)}, f32[30,34,1]{1,2,0:T(1,128)S(1)}, u32[]{:S(2)}, u32[]{:S(2)}) collective-permute-start(f32[30,34,1]{1,2,0:T(1,128)S(1)} %copy.141), channel_id=1, source_target_pairs={{0,1},{1,2},{2,3},{4,5},{5,6},{6,7},{8,9},{9,10},{10,11},{12,13},{... | collective-permute-start | bytes 12248 | tf_op jit(solution)/shard_map/ppermute | solution.py:28
  137.7 5.6 %collective-permute-start.12 = (f32[30,34,1]{1,2,0:T(1,128)S(1)}, f32[30,34,1]{1,2,0:T(1,128)S(1)}, u32[]{:S(2)}, u32[]{:S(2)}) collective-permute-start(f32[30,34,1]{1,2,0:T(1,128)S(1)} %copy.142), channel_id=1, source_target_pairs={{1,0},{2,1},{3,2},{5,4},{6,5},{7,6},{9,8},{10,9},{11,10},{13,12},{... | collective-permute-start | bytes 12248 | tf_op jit(solution)/shard_map/ppermute | solution.py:31
  144.4 2.5 %copy-start.16 = (f32[30,32,256]{2,1,0:T(8,128)S(1)}, f32[30,32,256]{2,1,0:T(8,128)}, u32[]{:S(2)}) copy-start(f32[30,32,256]{2,1,0:T(8,128)} %get-tuple-element.161) | copy-start | bytes 2949124
  176.1 25.0 %copy-start.4 = (f32[30,32,256]{2,1,0:T(8,128)}, f32[30,32,256]{2,1,0:T(8,128)S(1)}, u32[]{:S(2)}) copy-start(f32[30,32,256]{2,1,0:T(8,128)S(1)} %subtract_divide_fusion) | copy-start | bytes 2949124
  176.1 3.6 %collective-permute-start.13 = (f32[30,1,256]{2,1,0:T(1,128)S(1)}, f32[30,1,256]{2,1,0:T(1,128)S(1)}, u32[]{:S(2)}, u32[]{:S(2)}) collective-permute-start(f32[30,1,256]{2,1,0:T(1,128)S(1)} %get-tuple-element.177), channel_id=1, source_target_pairs={{0,4},{4,8},{8,12},{1,5},{5,9},{9,13},{2,6},{6,10},{10,14},{3,7},{... | collective-permute-start | bytes 92168 | tf_op jit(solution)/shard_map/ppermute | solution.py:28
  178.4 4.6 %collective-permute-start.14 = (f32[30,1,256]{2,1,0:T(1,128)S(1)}, f32[30,1,256]{2,1,0:T(1,128)S(1)}, u32[]{:S(2)}, u32[]{:S(2)}) collective-permute-start(f32[30,1,256]{2,1,0:T(1,128)S(1)} %get-tuple-element.178), channel_id=1, source_target_pairs={{4,0},{8,4},{12,8},{5,1},{9,5},{13,9},{6,2},{10,6},{14,10},{7,3},{... | collective-permute-start | bytes 92168 | tf_op jit(solution)/shard_map/ppermute | solution.py:31
  185.7 13.1 %collective-permute-start.15 = (f32[30,34,1]{1,2,0:T(1,128)S(1)}, f32[30,34,1]{1,2,0:T(1,128)S(1)}, u32[]{:S(2)}, u32[]{:S(2)}) collective-permute-start(f32[30,34,1]{1,2,0:T(1,128)S(1)} %copy.147), channel_id=1, source_target_pairs={{0,1},{1,2},{2,3},{4,5},{5,6},{6,7},{8,9},{9,10},{10,11},{12,13},{... | collective-permute-start | bytes 12248 | tf_op jit(solution)/shard_map/ppermute | solution.py:28
  190.8 9.1 %collective-permute-start.16 = (f32[30,34,1]{1,2,0:T(1,128)S(1)}, f32[30,34,1]{1,2,0:T(1,128)S(1)}, u32[]{:S(2)}, u32[]{:S(2)}) collective-permute-start(f32[30,34,1]{1,2,0:T(1,128)S(1)} %copy.148), channel_id=1, source_target_pairs={{1,0},{2,1},{3,2},{5,4},{6,5},{7,6},{9,8},{10,9},{11,10},{13,12},{... | collective-permute-start | bytes 12248 | tf_op jit(solution)/shard_map/ppermute | solution.py:31
  201.1 2.5 %copy-start.15 = (f32[30,32,256]{2,1,0:T(8,128)S(1)}, f32[30,32,256]{2,1,0:T(8,128)}, u32[]{:S(2)}) copy-start(f32[30,32,256]{2,1,0:T(8,128)} %get-tuple-element.160) | copy-start | bytes 2949124
  203.6 36.8 %copy-start.3 = (f32[1,30,32,256]{3,2,1,0:T(8,128)S(1)}, f32[1,30,32,256]{3,2,1,0:T(8,128)}, u32[]{:S(2)}) copy-start(f32[1,30,32,256]{3,2,1,0:T(8,128)} %param.29) | copy-start | bytes 2949124
  (11 other events, 24.4 us)
